TPU v7x, 128 devices: a whole 4x4x4 slice. The times are simulated.
128 devices in a mesh: fsdp: 32 (over y, z, core), dp: 4 (over x).
Axes of the slice: x: 4, y: 4, z: 4, core: 2. Of those that a mesh axis runs over, the one named last changes fastest.
Arguments:
- tokens: bfloat16 [16384, 4096], P(('fsdp', 'dp')), may hold values from -6 to 6
- gain: float32 [4096], replicated, may hold values from 0.5 to 1.5
- tiles: bfloat16 [512, 128, 128], P('fsdp'), may hold values from -0.25 to 0.25
- tile_rows: int32 [512], replicated, may hold values from 0 to 31, as said below
- tile_cols: int32 [512], replicated, may hold values from 0 to 111, as said below
- cotangent: bfloat16 [16384, 14336], P(('fsdp', 'dp')), may hold values from -6 to 6
Outputs:
- projected: bfloat16 [16384, 14336], P(('fsdp', 'dp'))
- token_grad: bfloat16 [16384, 4096], P(('fsdp', 'dp'))
- tile_grad: float32 [512, 128, 128], P('fsdp')
- gain_grad: float32 [4096], replicated
Inputs may be any that keep to these rules, and one draw needn't show every extreme that they name: The pairs (tile_rows[i], tile_cols[i]) are all different. `tile_cols`: pairs with tile_rows as above.
All inputs are finite; a program needn't handle non-finite values.
Results may differ from a plain program's by a relative error of at most 0.0049.
Values may be sent and summed in bfloat16 or wider, within the bound.
No kernel may reach another device: no remote copies, remote signals or barrier semaphores. Data moves between devices by JAX's collectives and lax.ppermute only.
A program may use at most 256 MiB of HBM per device.

v0:
```python
import jax
import jax.numpy as jnp
from jax import lax
from jax.sharding import PartitionSpec as P


def shards(tokens, gain, tiles, tile_rows, tile_cols, cotangent):
    count = tokens.shape[0]
    width = tokens.shape[1]
    tile = tiles.shape[1]
    row_blocks = width // tile
    col_blocks = cotangent.shape[1] // tile
    x32 = tokens.astype(jnp.float32)
    scale = lax.rsqrt(jnp.mean(x32 * x32, axis=-1, keepdims=True) + 1e-05)
    normed = (x32 * scale * gain).astype(jnp.bfloat16)
    xblocks = normed.reshape(count, row_blocks, tile)
    gblocks = cotangent.reshape(count, col_blocks, tile)
    piece = lax.all_gather(tiles, "fsdp", axis=0, tiled=True)
    rows = tile_rows
    cols = tile_cols
    xsel = jnp.take(xblocks, rows, axis=1)
    gsel = jnp.take(gblocks, cols, axis=1)
    forward = jnp.einsum("tkj,kjm->tkm", xsel, piece, preferred_element_type=jnp.float32)
    backward = jnp.einsum("tkm,kjm->tkj", gsel, piece, preferred_element_type=jnp.float32)
    stacked = jnp.stack([forward, backward], axis=0)
    outsum = jnp.zeros((count, col_blocks, tile), jnp.float32).at[:, tile_cols].add(stacked[0])
    back = jnp.zeros((count, row_blocks, tile), jnp.float32).at[:, tile_rows].add(stacked[1])
    projected = outsum.reshape(count, col_blocks * tile).astype(jnp.bfloat16)
    dnormed = back.reshape(count, width)
    gain_grad = lax.psum(jnp.sum(dnormed * x32 * scale, axis=0), ("fsdp", "dp"))
    inner = jnp.mean(x32 * gain * dnormed, axis=-1, keepdims=True)
    token_grad = (scale * gain * dnormed - x32 * scale**3 * inner).astype(jnp.bfloat16)
    group = tiles.shape[0]
    number = tiles.shape[0] * lax.axis_size("fsdp")

    def group_terms(first):
        rows = lax.dynamic_slice_in_dim(tile_rows, first, group, 0)
        cols = lax.dynamic_slice_in_dim(tile_cols, first, group, 0)
        xsel = jnp.take(xblocks, rows, axis=1)
        gsel = jnp.take(gblocks, cols, axis=1)
        return jnp.einsum("tkj,tkm->kjm", xsel, gsel, preferred_element_type=jnp.float32)

    firsts = group * jnp.arange(number // group, dtype=jnp.int32)
    result = lax.map(group_terms, firsts)
    owned = lax.psum_scatter(
        result.reshape(number, tile, tile), "fsdp", scatter_dimension=0, tiled=True
    )
    tile_grad = lax.psum(owned, "dp")
    return (projected, token_grad, tile_grad, gain_grad)


def solution(mesh):
    placed = (
        P(("fsdp", "dp"), None),
        P(),
        P("fsdp", None, None),
        P(),
        P(),
        P(("fsdp", "dp"), None),
    )
    return jax.shard_map(
        shards,
        mesh=mesh,
        in_specs=placed,
        out_specs=(P(("fsdp", "dp"), None), P(("fsdp", "dp"), None), P("fsdp", None, None), P()),
        check_vma=False,
    )
```

profile of v0, /device:TPU:1, one launch (start us, length us, event | category | flops | bytes accessed | tf_op | source)
XLA Modules:
  0.0 814.4 jit_solution(1176212291491571832)
XLA Ops:
  8.0 6.1 copy.35
  14.0 6.0 copy.36
  21.7 16.2 %gather_fusion.3 = bf16[512,128,128]{2,1,0:T(8,128)(2,1)} fusion(bf16[128,112,128]{2,0,1:T(8,128)(2,1)} %copy.36, s32[1024]{0:T(1024)S(1)} %pad_clamp_fusion.2), kind=kCustom, calls=%fused_computation.3 | custom fusion | bytes 33556480 | tf_op jit(solution)/shard_map/jit(_take)/gather | solution.py:22
  38.5 48.0 %all-gather.2.cloned.1.call-done = bf16[512,128,128]{2,1,0:T(8,128)(2,1)} async-done(((bf16[16,128,128]{2,1,0:T(8,128)(2,1)}), bf16[512,128,128]{2,1,0:T(8,128)(2,1)}) %all-gather.2.cloned.1.call-update) | async-done | bytes 16777232 | tf_op jit(solution)/shard_map/all_gather | solution.py:18
  86.5 28.2 %fusion.9 = f32[512,128,128]{2,1,0:T(8,128)} fusion(bf16[512,128,128]{2,1,0:T(8,128)(2,1)} %all-gather.2.cloned.1.call-done, bf16[512,128,128]{2,1,0:T(8,128)(2,1)} %gather_fusion.3, pred[512]{0:T(512)(128)(4,1)S(1)} %compare_and_fusion.2), kind=kOutput, calls=%fused_computation.22 | convolution fusion | flops 2155872256 | bytes 67109376 | tf_op jit(solution)/shard_map/tkm,kjm->tkj/dot_general | solution.py:24
  115.0 66.1 %scatter_fusion.1 = f32[128,32,128]{2,0,1:T(8,128)S(1)} fusion(f32[128,32,128]{2,0,1:T(8,128)S(1)} %broadcast_in_dim.69, s32[512]{0:T(512)S(1)} %compare_select_fusion.2, f32[512,128,128]{2,1,0:T(8,128)} %fusion.9), kind=kCustom, calls=%fused_computation.5 | custom fusion | flops 8388608 | bytes 100665344 | tf_op jit(solution)/shard_map/scatter-add | solution.py:27
  185.5 2.8 fusion.24
  189.0 237.1 %while.10 = (s32[]{:T(128)}, f32[32,16,128,128]{3,2,1,0:T(8,128)}, s32[32]{0:T(128)S(1)}, s32[512]{0:T(512)S(1)}, bf16[128,32,128]{2,0,1:T(8,128)(2,1)S(1)}, /*i...) while((s32[]{:T(128)}, f32[32,16,128,128]{3,2,1,0:T(8,128)}, ...), condition=%wide.region_5.6_spmd, body=%wide.region_4.5_spmd.sunk | while | flops 67635392 | bytes 4203735 | solution.py:44
  191.6 2.7 gather_fusion
  199.0 2.7 gather_fusion
  206.5 2.7 gather_fusion
  213.9 2.7 gather_fusion
  228.7 2.7 gather_fusion
  250.9 2.7 gather_fusion
  317.6 2.7 gather_fusion
  325.0 2.7 gather_fusion
  347.2 2.7 gather_fusion
  354.6 2.7 gather_fusion
  362.0 2.7 gather_fusion
  376.9 2.7 gather_fusion
  391.7 2.7 gather_fusion
  399.1 2.7 gather_fusion
  421.3 2.7 gather_fusion
  426.4 15.0 %gather_fusion.2 = bf16[512,128,128]{2,1,0:T(8,128)(2,1)} fusion(bf16[128,32,128]{2,0,1:T(8,128)(2,1)S(1)} %get-tuple-element.182, s32[1024]{0:T(1024)S(1)} %pad_clamp_fusion.3), kind=kCustom, calls=%fused_computation.2 | custom fusion | bytes 33556480 | tf_op jit(solution)/shard_map/jit(_take)/gather | solution.py:21
  441.3 148.6 %reduce-scatter.2.cloned.1.call-done = f32[16,128,128]{2,1,0:T(8,128)} async-done(((f32[512,128,128]{2,1,0:T(8,128)}), f32[16,128,128]{2,1,0:T(8,128)}) %reduce-scatter.2.cloned.1.call-update) | async-done | bytes 1048592 | tf_op jit(solution)/shard_map/reduce_scatter | solution.py:45
  590.0 24.5 %fusion.11 = f32[512,128,128]{2,1,0:T(8,128)} fusion(bf16[512,128,128]{2,1,0:T(8,128)(2,1)} %all-gather.2.cloned.1.call-done, bf16[512,128,128]{2,1,0:T(8,128)(2,1)} %gather_fusion.2, pred[512]{0:T(512)(128)(4,1)S(1)} %compare_and_fusion.3), kind=kOutput, calls=%fused_computation.24 | convolution fusion | flops 2155872256 | bytes 67109376 | tf_op jit(solution)/shard_map/tkj,kjm->tkm/dot_general | solution.py:23
  614.5 3.8 broadcast_in_dim.64
  618.3 103.4 %scatter_fusion = f32[128,112,128]{2,0,1:T(8,128)} fusion(f32[128,112,128]{2,0,1:T(8,128)} %broadcast_in_dim.64, s32[512]{0:T(512)S(1)} %compare_select_fusion.3, f32[512,128,128]{2,1,0:T(8,128)} %fusion.11), kind=kCustom, calls=%fused_computation.4 | custom fusion | flops 8388608 | bytes 100665344 | tf_op jit(solution)/shard_map/scatter-add | solution.py:26
  721.7 5.8 convert_element_type.17
  727.5 6.1 copy.34
  733.6 6.1 copy.40
  741.0 64.6 %psum.15 = f32[4096]{0:T(1024)} all-reduce(f32[4096]{0:T(1024)S(1)} %get-tuple-element.68), channel_id=1, replica_groups=mesh['fsdp'=32,'dp'=4] {'fsdp','dp'}, use_global_device_ids=true, to_apply=%region_9.10 | all-reduce | flops 4096 | bytes 32768 | tf_op jit(solution)/shard_map/psum | solution.py:30
  (242 shorter events, 145.7 us)
Async XLA Ops:
  7.2 14.5 %copy-start.2 = (s32[512]{0:T(512)S(1)}, s32[512]{0:T(512)}, u32[]{:S(2)}) copy-start(s32[512]{0:T(512)} %param.12) | copy-start | bytes 6148
  7.2 79.4 %all-gather.2.cloned.1.call-start = ((), (), s32[]{:S(2)}) async-start(), calls=%async_computation.1 | async-start | bytes 17301504 | tf_op jit(solution)/shard_map/all_gather | solution.py:18
  7.9 582.1 %reduce-scatter.2.cloned.1.call-start = ((), (), s32[]{:S(2)}) async-start(), calls=%async_computation.2 | async-start | bytes 34603008 | tf_op jit(solution)/shard_map/reduce_scatter | solution.py:45
  21.7 16.8 %copy-start.3 = (s32[512]{0:T(512)S(1)}, s32[512]{0:T(512)}, u32[]{:S(2)}) copy-start(s32[512]{0:T(512)} %param.11) | copy-start | bytes 6148
  115.0 68.0 %copy-start.1 = (f32[4096]{0:T(1024)S(1)}, f32[4096]{0:T(1024)}, u32[]{:S(2)}) copy-start(f32[4096]{0:T(1024)} %param.9) | copy-start | bytes 49156
  426.1 379.5 %all-reduce.2.cloned.1.call-start = ((), (), s32[]{:S(2)}) async-start(), calls=%async_computation.3 | async-start | bytes 2097152 | tf_op jit(solution)/shard_map/psum | solution.py:48
  721.7 18.0 %copy-start = (bf16[128,4096]{0,1:T(8,128)(2,1)S(1)}, bf16[128,4096]{0,1:T(8,128)(2,1)}, u32[]{:S(2)}) copy-start(bf16[128,4096]{0,1:T(8,128)(2,1)} %get-tuple-element.90) | copy-start | bytes 3145732
Sparse Core Ops, SparseCore 0:
  10.3 76.2 all-gather.1
  426.2 163.6 reduce-scatter.1
  592.5 44.0 all-reduce.1
where the time goes:
time: 820 us; the launch traced here: 814 us
  waiting for transfers between devices  197 us (24%)
  local copies, waits for them, and re-layouts  192 us (23%)
  other arithmetic  184 us (22%)
  matrix products  98.3 us (12%)
  blocking collectives  64.6 us (8%)
  loops' own time  63.1 us (8%)
  between operations  13.9 us (2%)
    reduce_scatter x1, waiting for transfers between devices, shards(): lax.psum_scatter(result.reshape(number, tile, tile), 'fsdp', scatter_dime...  149 us
    scatter-add x1, other arithmetic, shards(): jnp.zeros((count, col_blocks, tile), jnp.float32).at[:, tile_cols]  103 us
    gather x32, local copies, waits for them, and re-layouts, group_terms(): gsel = jnp.take(gblocks, cols, axis=1)  85.9 us
    scatter-add x1, other arithmetic, shards(): jnp.zeros((count, row_blocks, tile), jnp.float32).at[:, tile_rows]  66.1 us
    psum x1, blocking collectives, shards(): gain_grad = lax.psum(jnp.sum(dnormed * x32 * scale, axis=0), ('fsdp', 'dp'))  64.6 us
    another operation x1, loops' own time, shards(): result = lax.map(group_terms, firsts)  63.1 us
    all_gather x1, waiting for transfers between devices, shards(): piece = lax.all_gather(tiles, 'fsdp', axis=0, tiled=True)  48 us
    dot_general x32, matrix products, group_terms(): jnp.einsum('tkj,tkm->kjm', xsel, gsel, preferred_element_type=jnp.float32)  45.6 us
  transfers between devices with their start and end apart: 3, of which 2 were waited for; matrix products, arithmetic and copies ran while one was open for 24% of the time, Pallas kernels for 0%

commit v1 on v0

--- a/solution.py
+++ b/solution.py
@@ -2,6 +2,12 @@
 import jax.numpy as jnp
 from jax import lax
 from jax.sharding import PartitionSpec as P
+
+
+def add_all(value, name):
+    parts = lax.all_gather(value, name, axis=0, tiled=False)
+    summed = parts.sum(axis=0)
+    return summed
 
 
 def shards(tokens, gain, tiles, tile_rows, tile_cols, cotangent):
@@ -27,7 +33,7 @@
     back = jnp.zeros((count, row_blocks, tile), jnp.float32).at[:, tile_rows].add(stacked[1])
     projected = outsum.reshape(count, col_blocks * tile).astype(jnp.bfloat16)
     dnormed = back.reshape(count, width)
-    gain_grad = lax.psum(jnp.sum(dnormed * x32 * scale, axis=0), ("fsdp", "dp"))
+    gain_grad = add_all(jnp.sum(dnormed * x32 * scale, axis=0), ("fsdp", "dp"))
     inner = jnp.mean(x32 * gain * dnormed, axis=-1, keepdims=True)
     token_grad = (scale * gain * dnormed - x32 * scale**3 * inner).astype(jnp.bfloat16)
     group = tiles.shape[0]

time: 820 us -> 758 us (0.924)
  blocking collectives: 64.6 us -> 0 us
    psum x1 -> x0, blocking collectives: 64.6 us -> none  [shards(): gain_grad = lax.psum(jnp.sum(dnormed * x32 * scale, axis=0), ('fsdp', 'dp'))]
    unnamed x13 -> x15, local copies, waits for them, and re-layouts: 17.4 us -> 16.4 us
  transfers between devices with their start and end apart: 3 -> 4, of which waited for: 2 -> 2; matrix products, arithmetic and copies ran while one was open for 24% -> 26% of each run, Pallas kernels for 0% -> 0%
where the time goes in v1:
time: 758 us; the launch traced here: 753 us
  waiting for transfers between devices  198 us (26%)
  local copies, waits for them, and re-layouts  193 us (25%)
  other arithmetic  186 us (25%)
  matrix products  98.3 us (13%)
  loops' own time  63.1 us (8%)
  between operations  13.9 us (2%)
    reduce_scatter x1, waiting for transfers between devices, shards(): lax.psum_scatter(result.reshape(number, tile, tile), 'fsdp', scatter_dime...  148 us
    scatter-add x1, other arithmetic, shards(): jnp.zeros((count, col_blocks, tile), jnp.float32).at[:, tile_cols]  104 us
    gather x32, local copies, waits for them, and re-layouts, group_terms(): gsel = jnp.take(gblocks, cols, axis=1)  85.9 us
    scatter-add x1, other arithmetic, shards(): jnp.zeros((count, row_blocks, tile), jnp.float32).at[:, tile_rows]  66.1 us
    another operation x1, loops' own time, shards(): result = lax.map(group_terms, firsts)  63.1 us
    all_gather x1, waiting for transfers between devices, shards(): piece = lax.all_gather(tiles, 'fsdp', axis=0, tiled=True)  49.1 us
    dot_general x32, matrix products, group_terms(): jnp.einsum('tkj,tkm->kjm', xsel, gsel, preferred_element_type=jnp.float32)  45.6 us
    dot_general x1, matrix products, shards(): jnp.einsum('tkm,kjm->tkj', gsel, piece, preferred_element_type=jnp.float32)  28.2 us
  transfers between devices with their start and end apart: 4, of which 2 were waited for; matrix products, arithmetic and copies ran while one was open for 26% of the time, Pallas kernels for 0%

profile of v1, /device:TPU:1, one launch (start us, length us, event | category | flops | bytes accessed | tf_op | source)
XLA Modules:
  0.0 753.0 jit_solution(3270237624664294753)
XLA Ops:
  8.0 6.1 copy.46
  14.0 6.0 copy.47
  20.8 16.1 %gather_fusion.3 = bf16[512,128,128]{2,1,0:T(8,128)(2,1)} fusion(bf16[128,112,128]{2,0,1:T(8,128)(2,1)} %copy.47, s32[1024]{0:T(1024)S(1)} %pad_clamp_fusion.2), kind=kCustom, calls=%fused_computation.3 | custom fusion | bytes 33556480 | tf_op jit(solution)/shard_map/jit(_take)/gather | solution.py:28
  37.5 49.1 %all-gather.4.cloned.1.call-done = bf16[512,128,128]{2,1,0:T(8,128)(2,1)} async-done(((bf16[16,128,128]{2,1,0:T(8,128)(2,1)}), bf16[512,128,128]{2,1,0:T(8,128)(2,1)}) %all-gather.4.cloned.1.call-update) | async-done | bytes 16777232 | tf_op jit(solution)/shard_map/all_gather | solution.py:24
  86.6 28.2 %fusion.9 = f32[512,128,128]{2,1,0:T(8,128)} fusion(bf16[512,128,128]{2,1,0:T(8,128)(2,1)} %all-gather.4.cloned.1.call-done, bf16[512,128,128]{2,1,0:T(8,128)(2,1)} %gather_fusion.3, pred[512]{0:T(512)(128)(4,1)S(1)} %compare_and_fusion.2), kind=kOutput, calls=%fused_computation.22 | convolution fusion | flops 2155872256 | bytes 67109376 | tf_op jit(solution)/shard_map/tkm,kjm->tkj/dot_general | solution.py:30
  115.0 66.1 %scatter_fusion.1 = f32[128,32,128]{2,0,1:T(8,128)S(1)} fusion(f32[128,32,128]{2,0,1:T(8,128)S(1)} %broadcast_in_dim.69, s32[512]{0:T(512)S(1)} %compare_select_fusion.2, f32[512,128,128]{2,1,0:T(8,128)} %fusion.9), kind=kCustom, calls=%fused_computation.5 | custom fusion | flops 8388608 | bytes 100665344 | tf_op jit(solution)/shard_map/scatter-add | solution.py:33
  183.0 3.1 fusion.28
  186.1 2.8 fusion.24
  189.6 237.1 %while.10 = (s32[]{:T(128)}, f32[32,16,128,128]{3,2,1,0:T(8,128)}, s32[32]{0:T(128)S(1)}, s32[512]{0:T(512)S(1)}, bf16[128,32,128]{2,0,1:T(8,128)(2,1)S(1)}, /*i...) while((s32[]{:T(128)}, f32[32,16,128,128]{3,2,1,0:T(8,128)}, ...), condition=%wide.region_5.6_spmd, body=%wide.region_4.5_spmd.sunk | while | flops 67635392 | bytes 4203735 | solution.py:50
  192.2 2.7 gather_fusion
  199.6 2.7 gather_fusion
  214.5 2.7 gather_fusion
  221.9 2.7 gather_fusion
  229.2 2.7 gather_fusion
  236.7 2.7 gather_fusion
  266.3 2.7 gather_fusion
  273.7 2.7 gather_fusion
  281.1 2.7 gather_fusion
  296.0 2.7 gather_fusion
  303.4 2.7 gather_fusion
  310.8 2.7 gather_fusion
  325.6 2.7 gather_fusion
  333.0 2.7 gather_fusion
  340.4 2.7 gather_fusion
  427.7 15.0 %gather_fusion.2 = bf16[512,128,128]{2,1,0:T(8,128)(2,1)} fusion(bf16[128,32,128]{2,0,1:T(8,128)(2,1)S(1)} %get-tuple-element.194, s32[1024]{0:T(1024)S(1)} %pad_clamp_fusion.3), kind=kCustom, calls=%fused_computation.2 | custom fusion | bytes 33556480 | tf_op jit(solution)/shard_map/jit(_take)/gather | solution.py:27
  442.6 147.7 %reduce-scatter.2.cloned.1.call-done = f32[16,128,128]{2,1,0:T(8,128)} async-done(((f32[512,128,128]{2,1,0:T(8,128)}), f32[16,128,128]{2,1,0:T(8,128)}) %reduce-scatter.2.cloned.1.call-update) | async-done | bytes 1048592 | tf_op jit(solution)/shard_map/reduce_scatter | solution.py:51
  590.4 24.4 %fusion.11 = f32[512,128,128]{2,1,0:T(8,128)} fusion(bf16[512,128,128]{2,1,0:T(8,128)(2,1)} %all-gather.4.cloned.1.call-done, bf16[512,128,128]{2,1,0:T(8,128)(2,1)} %gather_fusion.2, pred[512]{0:T(512)(128)(4,1)S(1)} %compare_and_fusion.3), kind=kOutput, calls=%fused_computation.24 | convolution fusion | flops 2155872256 | bytes 67109376 | tf_op jit(solution)/shard_map/tkj,kjm->tkm/dot_general | solution.py:29
  614.8 3.8 broadcast_in_dim.64
  618.7 103.7 %scatter_fusion = f32[128,112,128]{2,0,1:T(8,128)} fusion(f32[128,112,128]{2,0,1:T(8,128)} %broadcast_in_dim.64, s32[512]{0:T(512)S(1)} %compare_select_fusion.3, f32[512,128,128]{2,1,0:T(8,128)} %fusion.11), kind=kCustom, calls=%fused_computation.4 | custom fusion | flops 8388608 | bytes 100665344 | tf_op jit(solution)/shard_map/scatter-add | solution.py:32
  722.4 5.8 convert_element_type.17
  728.1 6.2 copy.45
  734.3 6.1 copy.51
  (248 shorter events, 145.4 us)
Async XLA Ops:
  7.2 12.9 %copy-start.1 = (bf16[128,4096]{1,0:T(8,128)(2,1)S(1)}, bf16[128,4096]{1,0:T(8,128)(2,1)}, u32[]{:S(2)}) copy-start(bf16[128,4096]{1,0:T(8,128)(2,1)} %param.8) | copy-start | bytes 3145732
  7.2 79.4 %all-gather.4.cloned.1.call-start = ((), (), s32[]{:S(2)}) async-start(), calls=%async_computation.1 | async-start | bytes 17301504 | tf_op jit(solution)/shard_map/all_gather | solution.py:24
  7.9 582.5 %reduce-scatter.2.cloned.1.call-start = ((), (), s32[]{:S(2)}) async-start(), calls=%async_computation.2 | async-start | bytes 34603008 | tf_op jit(solution)/shard_map/reduce_scatter | solution.py:51
  8.0 12.8 %copy-start.3 = (s32[512]{0:T(512)S(1)}, s32[512]{0:T(512)}, u32[]{:S(2)}) copy-start(s32[512]{0:T(512)} %param.12) | copy-start | bytes 6148
  20.8 16.7 %copy-start.4 = (s32[512]{0:T(512)S(1)}, s32[512]{0:T(512)}, u32[]{:S(2)}) copy-start(s32[512]{0:T(512)} %param.11) | copy-start | bytes 6148
  115.0 68.0 %copy-start.2 = (f32[4096]{0:T(1024)S(1)}, f32[4096]{0:T(1024)}, u32[]{:S(2)}) copy-start(f32[4096]{0:T(1024)} %param.9) | copy-start | bytes 49156
  426.7 315.0 %all-gather.6.cloned.1.call-start = ((), (), s32[]{:S(2)}) async-start(), calls=%async_computation.4 | async-start | bytes 2113536 | tf_op jit(solution)/shard_map/all_gather | solution.py:8
  427.4 316.7 %all-reduce.2.cloned.1.call-start = ((), (), s32[]{:S(2)}) async-start(), calls=%async_computation.3 | async-start | bytes 2097152 | tf_op jit(solution)/shard_map/psum | solution.py:54
  728.1 12.2 %copy-start = (bf16[128,4096]{0,1:T(8,128)(2,1)S(1)}, bf16[128,4096]{0,1:T(8,128)(2,1)}, u32[]{:S(2)}) copy-start(bf16[128,4096]{0,1:T(8,128)(2,1)} %get-tuple-element.101) | copy-start | bytes 3145732
Sparse Core Ops, SparseCore 0:
  10.3 76.2 all-gather.3
  426.8 163.5 reduce-scatter.1
  594.4 65.5 all-gather.5
  662.3 41.3 all-reduce.1
